TPU v7x, 256 devices: a whole 4x4x8 slice. The times are simulated.
256 devices in a mesh: section: 8 (over y, core), ctx: 32 (over z, x).
Axes of the slice: x: 4, y: 4, z: 8, core: 2. Of those that a mesh axis runs over, the one named last changes fastest.
Arguments:
- section_input: bfloat16 [2, 4096, 2048], P(None, 'ctx'), may hold values from -6 to 6
- cotangent: bfloat16 [2, 4096, 2048], P(None, 'ctx'), may hold values from -6 to 6
- w_query: bfloat16 [8, 2048, 1024], P('section', 'ctx'), may hold values from -0.125 to 0.125
- w_key: bfloat16 [8, 2048, 1024], P('section', 'ctx'), may hold values from -0.125 to 0.125
- w_value: bfloat16 [8, 2048, 1024], P('section', 'ctx'), may hold values from -0.125 to 0.125
- w_out: bfloat16 [8, 1024, 2048], P('section', 'ctx'), may hold values from -0.1875 to 0.1875
- block_mask: int32 [2, 128, 2], P(None, 'ctx'), may hold values 0 or 1
Outputs:
- section_output: bfloat16 [8, 2, 4096, 2048], P('section', None, 'ctx')
- input_grad: bfloat16 [8, 2, 4096, 2048], P('section', None, 'ctx')
Inputs may be any that keep to these rules, and one draw needn't show every extreme that they name: A block always attends to itself; column 0 and 1 of block_mask choose its two neighbour blocks.
All inputs are finite; a program needn't handle non-finite values.
Results may differ from a plain program's by a relative error of at most 0.03.
Values may be sent and summed in bfloat16 or wider, within the bound.
No kernel may reach another device: no remote copies, remote signals or barrier semaphores. Data moves between devices by JAX's collectives and lax.ppermute only.
A program may use at most 128 MiB of HBM per device.

v0:
```python
import jax
import jax.numpy as jnp
from jax import lax
from jax.sharding import PartitionSpec as P

D = 2048
HEADS = 8
HDIM = 128
BLOCKS_DEV = 4
BLK = 32


def padded(block, sides, width):
    for axis, dim in sides:
        count = lax.axis_size(axis)
        forward = [(i, i + 1) for i in range(count - 1)]
        backward = [(target, source) for source, target in forward]
        low = lax.ppermute(
            lax.slice_in_dim(block, block.shape[dim] - width, None, axis=dim), axis, forward
        )
        high = lax.ppermute(lax.slice_in_dim(block, 0, width, axis=dim), axis, backward)
        block = jnp.concatenate([low, block, high], axis=dim)
    return block


def shifted(block, axis, distance):
    devices = range(lax.axis_size(axis))
    route = [(i - distance, i) for i in devices if i - distance in devices]
    return lax.ppermute(block, axis, route)


def rms_scale(values):
    return values * lax.rsqrt(jnp.mean(values * values, axis=-1, keepdims=True) + 1e-06)


def allowed_keys(mask_rows, block_ids, block_count):
    mask_float = mask_rows.astype(jnp.float32)
    left = mask_float[:, 0] * (block_ids > 0).astype(jnp.float32)
    right = mask_float[:, 1] * (block_ids < block_count - 1).astype(jnp.float32)
    return jnp.stack([left, jnp.ones_like(left), right], axis=1)


def project(layer_in, w_query, w_key, w_value):
    length = layer_in.shape[0]
    normed = rms_scale(layer_in.astype(jnp.float32)).astype(jnp.bfloat16)

    def head_normed(weight):
        out = jnp.dot(normed, weight, preferred_element_type=jnp.float32)
        out = rms_scale(out.reshape(length, HEADS, HDIM))
        return out.reshape(length, HEADS * HDIM).astype(jnp.bfloat16)

    query = head_normed(w_query)
    key = head_normed(w_key)
    value = jnp.dot(normed, w_value, preferred_element_type=jnp.float32).astype(jnp.bfloat16)
    return (query, key, value)


def attend(query, keys_ext, values_ext, allow, layer_in, w_out):
    length = query.shape[0]
    nblock = length // BLK
    queries = query.reshape(nblock, BLK, HEADS, HDIM)

    def windows(extended):
        grid = extended.reshape(nblock + 2, BLK, HEADS, HDIM)
        return jnp.concatenate([grid[:-2], grid[1:-1], grid[2:]], axis=1)

    keys = windows(keys_ext)
    values = windows(values_ext)
    scores = jnp.einsum(
        "bqhd,bkhd->bhqk", queries, keys, preferred_element_type=jnp.float32
    ) * HDIM ** (-0.5)
    weight = jnp.repeat(allow, BLK, axis=1)[:, None, None, :]
    probs = jnp.exp(scores) * weight
    total = jnp.sum(probs, axis=-1)
    attended = jnp.einsum(
        "bhqk,bkhd->bqhd", probs.astype(jnp.bfloat16), values, preferred_element_type=jnp.float32
    )
    attended = attended / jnp.transpose(total, (0, 2, 1))[..., None]
    attended = attended.reshape(length, HEADS * HDIM).astype(jnp.bfloat16)
    update = jnp.dot(attended, w_out, preferred_element_type=jnp.float32)
    return (layer_in.astype(jnp.float32) + update).astype(jnp.bfloat16)


def put_slot(buffer, value, slot, active):
    return jnp.where(active, lax.dynamic_update_index_in_dim(buffer, value, slot, 0), buffer)


def take_slot(buffer, slot):
    return lax.dynamic_index_in_dim(buffer, slot, 0, keepdims=False)


def per_device(section_input, cotangent, w_query, w_key, w_value, w_out, block_mask):
    n_section = lax.axis_size("section")
    n_ctx = lax.axis_size("ctx")
    section = lax.axis_index("section")
    place = lax.axis_index("ctx")
    micro = section_input.shape[0]
    length = section_input.shape[1]
    width = HEADS * HDIM
    full_query, full_key, full_value, full_out = (
        lax.all_gather(w_query[0], "ctx", axis=0, tiled=True),
        lax.all_gather(w_key[0], "ctx", axis=0, tiled=True),
        lax.all_gather(w_value[0], "ctx", axis=0, tiled=True),
        lax.all_gather(w_out[0], "ctx", axis=0, tiled=True),
    )
    block_ids = place * BLOCKS_DEV + jnp.arange(BLOCKS_DEV)
    allows = jax.vmap(lambda rows_mask: allowed_keys(rows_mask, block_ids, BLOCKS_DEV * n_ctx))(
        block_mask
    )
    zero_rows = jnp.zeros((length, D), jnp.bfloat16)
    zero_heads = jnp.zeros((length, width), jnp.bfloat16)
    zero_wide = jnp.zeros((length + 2 * BLK, width), jnp.bfloat16)
    steps_total = n_section + micro - 1

    def run_project(values):
        return project(values, full_query, full_key, full_value)

    def skip_project(values):
        return (zero_heads, zero_heads, zero_heads)

    def run_attend(query, extended, layer_in, allow):
        return attend(query, extended[0], extended[1], allow, layer_in, full_out)

    def skip_attend(query, extended, layer_in, allow):
        return zero_rows

    kv_store = jnp.zeros((micro, 2, length, width), jnp.bfloat16)
    inputs = jnp.zeros((micro, length, D), jnp.bfloat16)
    outputs = jnp.zeros((micro, length, D), jnp.bfloat16)
    queries = jnp.zeros((micro, length, width), jnp.bfloat16)

    def forward_step(step, carry):
        incoming, inputs, outputs, queries, kv_store = carry
        micro_id = step - section
        active = (micro_id >= 0) & (micro_id < micro)
        slot = jnp.clip(micro_id, 0, micro - 1)
        layer_in = jnp.where(section == 0, take_slot(section_input, slot), incoming)
        query, key, value = lax.cond(active, run_project, skip_project, layer_in)
        local_kv = jnp.stack([key, value])
        extended = padded(local_kv, (("ctx", 1),), BLK)
        allow = take_slot(allows, slot)
        result = lax.cond(active, run_attend, skip_attend, query, extended, layer_in, allow)
        inputs = put_slot(inputs, layer_in, slot, active)
        outputs = put_slot(outputs, result, slot, active)
        queries = put_slot(queries, query, slot, active)
        kv_store = put_slot(kv_store, local_kv, slot, active)
        incoming = shifted(result, "section", 1)
        return (incoming, inputs, outputs, queries, kv_store)

    carry = (zero_rows, inputs, outputs, queries, kv_store)
    _, inputs, outputs, queries, kv_store = lax.fori_loop(0, steps_total, forward_step, carry)

    def pull_attend(query, extended, layer_in, allow, grad_in):

        def local_attend(query_in, keys_in, values_in, rows_in):
            return attend(query_in, keys_in, values_in, allow, rows_in, full_out)

        _, pull = jax.vjp(local_attend, query, extended[0], extended[1], layer_in)
        return pull(grad_in)

    def skip_pull(query, extended, layer_in, allow, grad_in):
        return (zero_heads, zero_wide, zero_wide, zero_rows)

    def pull_project(layer_in, d_query, own):
        _, pull = jax.vjp(run_project, layer_in)
        return pull((d_query, own[0], own[1]))[0]

    def skip_pull_project(layer_in, d_query, own):
        return zero_rows

    grads = jnp.zeros((micro, length, D), jnp.bfloat16)

    def backward_step(step, carry):
        incoming, grads = carry
        micro_id = step - (n_section - 1 - section)
        active = (micro_id >= 0) & (micro_id < micro)
        slot = jnp.clip(micro_id, 0, micro - 1)
        grad_in = jnp.where(section == n_section - 1, take_slot(cotangent, slot), incoming)
        layer_in = take_slot(inputs, slot)
        query = take_slot(queries, slot)
        extended = padded(take_slot(kv_store, slot), (("ctx", 1),), BLK)
        allow = take_slot(allows, slot)
        d_query, d_keys, d_values, d_direct = lax.cond(
            active, pull_attend, skip_pull, query, extended, layer_in, allow, grad_in
        )
        d_wide = jnp.stack([d_keys, d_values])
        rims = jnp.concatenate([d_wide[:, :BLK], d_wide[:, -BLK:]], axis=1)
        returned = padded(rims, (("ctx", 1),), BLK)
        own = d_wide[:, BLK:-BLK]
        own = own.at[:, :BLK].add(returned[:, :BLK])
        own = own.at[:, -BLK:].add(returned[:, -BLK:])
        d_projected = lax.cond(active, pull_project, skip_pull_project, layer_in, d_query, own)
        d_input = d_direct + d_projected
        grads = put_slot(grads, d_input, slot, active)
        incoming = shifted(d_input, "section", -1)
        return (incoming, grads)

    _, grads = lax.fori_loop(0, steps_total, backward_step, (zero_rows, grads))
    return (outputs[None], grads[None])


def solution(mesh):
    return jax.shard_map(
        per_device,
        mesh=mesh,
        in_specs=(
            P(None, "ctx", None),
            P(None, "ctx", None),
            P("section", "ctx", None),
            P("section", "ctx", None),
            P("section", "ctx", None),
            P("section", "ctx", None),
            P(None, "ctx", None),
        ),
        out_specs=(P("section", None, "ctx", None), P("section", None, "ctx", None)),
        check_vma=False,
    )
```

profile of v0, /device:TPU:103, one launch (start us, length us, event | category | flops | bytes accessed | tf_op | source)
XLA Modules:
  0.0 1315.3 jit_solution(2852460559565105699)
XLA Ops:
  11.0 78.0 %all-gather.9.cloned.1.call-done = bf16[1,2048,1024]{2,1,0:T(8,128)(2,1)} async-done(((bf16[1,64,1024]{2,1,0:T(8,128)(2,1)}), bf16[1,2048,1024]{2,1,0:T(8,128)(2,1)}) %all-gather.9.cloned.1.call-update) | async-done | bytes 4194320 | tf_op jit(solution)/shard_map/all_gather | solution.py:101
  88.9 81.8 %all-gather.11.cloned.1.call-done = bf16[1,2048,1024]{2,1,0:T(8,128)(2,1)} async-done(((bf16[1,64,1024]{2,1,0:T(8,128)(2,1)}), bf16[1,2048,1024]{2,1,0:T(8,128)(2,1)}) %all-gather.11.cloned.1.call-update) | async-done | bytes 4194320 | tf_op jit(solution)/shard_map/all_gather | solution.py:102
  170.7 81.8 %all-gather.13.cloned.1.call-done = bf16[1,2048,1024]{2,1,0:T(8,128)(2,1)} async-done(((bf16[1,64,1024]{2,1,0:T(8,128)(2,1)}), bf16[1,2048,1024]{2,1,0:T(8,128)(2,1)}) %all-gather.13.cloned.1.call-update) | async-done | bytes 4194320 | tf_op jit(solution)/shard_map/all_gather | solution.py:103
  252.5 81.6 %all-gather.15.cloned.1.call-done = bf16[1,1024,2048]{2,1,0:T(8,128)(2,1)} async-done(((bf16[1,32,2048]{2,1,0:T(8,128)(2,1)}), bf16[1,1024,2048]{2,1,0:T(8,128)(2,1)}) %all-gather.15.cloned.1.call-update) | async-done | bytes 4194320 | tf_op jit(solution)/shard_map/all_gather | solution.py:104
  337.4 301.7 %while.41 = (s32[]{:T(128)}, bf16[128,2048]{1,0:T(8,128)(2,1)S(1)}, bf16[2,128,2048]{2,1,0:T(8,128)(2,1)S(1)}, bf16[2,128,2048]{2,1,0:T(8,128)(2,1)}, bf16[2,128...) while((s32[]{:T(128)}, bf16[128,2048]{1,0:T(8,128)(2,1)S(1)}, ...), condition=%wide.region_9.10_spmd, body=%wide.region_0.9_spmd.sunk | while | flops 2211841024 | bytes 75189416 | solution.py:151
  350.6 7.9 collective-permute-start.2
  362.1 12.5 collective-permute-done.2
  376.0 10.8 conditional.8
  388.8 7.4 collective-permute-start.1
  414.6 10.8 conditional.8
  458.0 7.4 collective-permute-start.1
  468.4 21.3 %collective-permute-start.2 = (bf16[128,2048]{1,0:T(8,128)(2,1)}, bf16[128,2048]{1,0:T(8,128)(2,1)S(1)}, u32[]{:S(2)}, u32[]{:S(2)}) collective-permute-start(bf16[128,2048]{1,0:T(8,128)(2,1)} %get-tuple-element.1251), channel_id=1, source_target_pairs={{0,32},{32,64},{64,96},{96,128},{128,160},{160,192},{192,224},{1,3... | collective-permute-start | bytes 1572872 | tf_op jit(solution)/shard_map/while/body/eval_jaxpr/ppermute | solution.py:29
  499.6 7.4 collective-permute-start.1
  525.0 7.4 collective-permute-start.1
  535.4 8.4 collective-permute-start.2
  553.7 7.4 collective-permute-start.1
  579.1 7.4 collective-permute-start.1
  589.5 17.8 %collective-permute-start.2 = (bf16[128,2048]{1,0:T(8,128)(2,1)}, bf16[128,2048]{1,0:T(8,128)(2,1)S(1)}, u32[]{:S(2)}, u32[]{:S(2)}) collective-permute-start(bf16[128,2048]{1,0:T(8,128)(2,1)} %get-tuple-element.1251), channel_id=1, source_target_pairs={{0,32},{32,64},{64,96},{96,128},{128,160},{160,192},{192,224},{1,3... | collective-permute-start | bytes 1572872 | tf_op jit(solution)/shard_map/while/body/eval_jaxpr/ppermute | solution.py:29
  617.2 7.4 collective-permute-start.1
  641.0 667.8 %while.42 = (s32[]{:T(128)}, bf16[128,2048]{1,0:T(8,128)(2,1)}, bf16[2,128,2048]{2,1,0:T(8,128)(2,1)}, s32[]{:T(128)}, bf16[2,2,128,1024]{3,2,1,0:T(8,128)(2,1)}...) while((s32[]{:T(128)}, bf16[128,2048]{1,0:T(8,128)(2,1)}, ...), condition=%wide.region_24.25_spmd, body=%wide.region_10.24_spmd.sunk | while | flops 3389073152 | bytes 170649296 | solution.py:198
  644.1 7.4 collective-permute-start.4
  655.5 7.1 collective-permute-start.5
  664.5 7.1 collective-permute-done.6
  675.7 15.2 %collective-permute-done.7 = bf16[128,2048]{1,0:T(8,128)(2,1)S(1)} collective-permute-done((bf16[128,2048]{1,0:T(8,128)(2,1)S(1)}, bf16[128,2048]{1,0:T(8,128)(2,1)S(1)}, u32[]{:S(2)}, u32[]{:S(2)}) %collective-permute-start.7) | collective-permute-done | bytes 524320 | tf_op jit(solution)/shard_map/while/body/eval_jaxpr/ppermute | solution.py:29
  706.5 7.1 collective-permute-start.5
  715.6 7.1 collective-permute-done.6
  726.8 9.4 collective-permute-done.7
  750.7 7.1 collective-permute-start.5
  759.8 7.1 collective-permute-done.6
  771.0 22.7 %collective-permute-done.7 = bf16[128,2048]{1,0:T(8,128)(2,1)S(1)} collective-permute-done((bf16[128,2048]{1,0:T(8,128)(2,1)S(1)}, bf16[128,2048]{1,0:T(8,128)(2,1)S(1)}, u32[]{:S(2)}, u32[]{:S(2)}) %collective-permute-start.7) | collective-permute-done | bytes 524320 | tf_op jit(solution)/shard_map/while/body/eval_jaxpr/ppermute | solution.py:29
  808.2 7.1 collective-permute-start.5
  828.4 9.2 collective-permute-done.7
  852.2 7.1 collective-permute-start.5
  861.2 7.1 collective-permute-done.6
  872.5 14.1 %collective-permute-done.7 = bf16[128,2048]{1,0:T(8,128)(2,1)S(1)} collective-permute-done((bf16[128,2048]{1,0:T(8,128)(2,1)S(1)}, bf16[128,2048]{1,0:T(8,128)(2,1)S(1)}, u32[]{:S(2)}, u32[]{:S(2)}) %collective-permute-start.7) | collective-permute-done | bytes 524320 | tf_op jit(solution)/shard_map/while/body/eval_jaxpr/ppermute | solution.py:29
  901.7 7.4 collective-permute-start.5
  911.0 7.1 collective-permute-done.6
  922.3 176.7 %collective-permute-done.7 = bf16[128,2048]{1,0:T(8,128)(2,1)S(1)} collective-permute-done((bf16[128,2048]{1,0:T(8,128)(2,1)S(1)}, bf16[128,2048]{1,0:T(8,128)(2,1)S(1)}, u32[]{:S(2)}, u32[]{:S(2)}) %collective-permute-start.7) | collective-permute-done | bytes 524320 | tf_op jit(solution)/shard_map/while/body/eval_jaxpr/ppermute | solution.py:29
  1111.5 11.2 conditional.10
  1124.6 7.1 collective-permute-start.5
  1140.7 18.6 %conditional.11 = (bf16[128,2048]{1,0:T(8,128)(2,1)S(1)}) conditional(s32[]{:T(128)} %convert_element_type.302, () %tuple.209, (bf16[2,192,1024]{2,1,0:T(8,128)(2,1)S(1)}, bf16[2,32,1024]{2,1,0:T(8,128)(2,1)S(1)}, bf16[2,32,1024]{2,1,0:T(8,128)(2,1)S(1)}, bf16[2048,1024]{1,0:T(8,128)(2,1)}, bf16[2,128,2048]{2,1,0:T(8,128)(2,1)S(1)}, ...), branch_computations={%region_15.15_spmd, %region_16.23_spmd} | conditional | flops 2693800704 | bytes 90314520 | solution.py:192
  1163.4 9.5 collective-permute-done.7
  1185.4 11.2 conditional.10
  1198.5 7.1 collective-permute-start.5
  1214.6 18.6 %conditional.11 = (bf16[128,2048]{1,0:T(8,128)(2,1)S(1)}) conditional(s32[]{:T(128)} %convert_element_type.302, () %tuple.209, (bf16[2,192,1024]{2,1,0:T(8,128)(2,1)S(1)}, bf16[2,32,1024]{2,1,0:T(8,128)(2,1)S(1)}, bf16[2,32,1024]{2,1,0:T(8,128)(2,1)S(1)}, bf16[2048,1024]{1,0:T(8,128)(2,1)}, bf16[2,128,2048]{2,1,0:T(8,128)(2,1)S(1)}, ...), branch_computations={%region_15.15_spmd, %region_16.23_spmd} | conditional | flops 2693800704 | bytes 90314520 | solution.py:192
  1237.4 8.6 collective-permute-done.7
  1260.4 7.1 collective-permute-start.5
  1278.8 27.7 %collective-permute-start.7 = (bf16[128,2048]{1,0:T(8,128)(2,1)S(1)}, bf16[128,2048]{1,0:T(8,128)(2,1)S(1)}, u32[]{:S(2)}, u32[]{:S(2)}) collective-permute-start(bf16[128,2048]{1,0:T(8,128)(2,1)S(1)} %get-tuple-element.1276), channel_id=1, source_target_pairs={{32,0},{64,32},{96,64},{128,96},{160,128},{192,160},{224,192},{33,... | collective-permute-start | bytes 1572872 | tf_op jit(solution)/shard_map/while/body/eval_jaxpr/ppermute | solution.py:29
  (696 shorter events, 476.1 us)
Async XLA Ops:
  7.2 81.8 %all-gather.9.cloned.1.call-start = ((), (), s32[]{:S(2)}) async-start(), calls=%async_computation | async-start | bytes 4325376 | tf_op jit(solution)/shard_map/all_gather | solution.py:101
  7.9 162.8 %all-gather.11.cloned.1.call-start = ((), (), s32[]{:S(2)}) async-start(), calls=%async_computation.1 | async-start | bytes 4325376 | tf_op jit(solution)/shard_map/all_gather | solution.py:102
  8.6 243.8 %all-gather.13.cloned.1.call-start = ((), (), s32[]{:S(2)}) async-start(), calls=%async_computation.2 | async-start | bytes 4325376 | tf_op jit(solution)/shard_map/all_gather | solution.py:103
  9.4 324.7 %all-gather.15.cloned.1.call-start = ((), (), s32[]{:S(2)}) async-start(), calls=%async_computation.3 | async-start | bytes 4325376 | tf_op jit(solution)/shard_map/all_gather | solution.py:104
  338.9 10.7 collective-permute-start
  350.6 24.1 %collective-permute-start.2 = (bf16[128,2048]{1,0:T(8,128)(2,1)}, bf16[128,2048]{1,0:T(8,128)(2,1)S(1)}, u32[]{:S(2)}, u32[]{:S(2)}) collective-permute-start(bf16[128,2048]{1,0:T(8,128)(2,1)} %get-tuple-element.1251), channel_id=1, source_target_pairs={{0,32},{32,64},{64,96},{96,128},{128,160},{160,192},{192,224},{1,3... | collective-permute-start | bytes 1572872 | tf_op jit(solution)/shard_map/while/body/eval_jaxpr/ppermute | solution.py:29
  386.9 11.4 collective-permute-start
  388.8 9.5 collective-permute-start.1
  425.5 11.0 collective-permute-start
  443.1 11.4 collective-permute-start.2
  456.0 11.4 collective-permute-start
  458.0 9.5 collective-permute-start.1
  468.4 27.8 %collective-permute-start.2 = (bf16[128,2048]{1,0:T(8,128)(2,1)}, bf16[128,2048]{1,0:T(8,128)(2,1)S(1)}, u32[]{:S(2)}, u32[]{:S(2)}) collective-permute-start(bf16[128,2048]{1,0:T(8,128)(2,1)} %get-tuple-element.1251), channel_id=1, source_target_pairs={{0,32},{32,64},{64,96},{96,128},{128,160},{160,192},{192,224},{1,3... | collective-permute-start | bytes 1572872 | tf_op jit(solution)/shard_map/while/body/eval_jaxpr/ppermute | solution.py:29
  497.7 11.4 collective-permute-start
  499.6 9.5 collective-permute-start.1
  510.1 11.4 collective-permute-start.2
  523.0 11.4 collective-permute-start
  525.0 9.5 collective-permute-start.1
  535.4 14.8 %collective-permute-start.2 = (bf16[128,2048]{1,0:T(8,128)(2,1)}, bf16[128,2048]{1,0:T(8,128)(2,1)S(1)}, u32[]{:S(2)}, u32[]{:S(2)}) collective-permute-start(bf16[128,2048]{1,0:T(8,128)(2,1)} %get-tuple-element.1251), channel_id=1, source_target_pairs={{0,32},{32,64},{64,96},{96,128},{128,160},{160,192},{192,224},{1,3... | collective-permute-start | bytes 1572872 | tf_op jit(solution)/shard_map/while/body/eval_jaxpr/ppermute | solution.py:29
  551.8 11.4 collective-permute-start
  553.7 9.5 collective-permute-start.1
  564.2 11.4 collective-permute-start.2
  577.1 11.4 collective-permute-start
  579.1 9.5 collective-permute-start.1
  589.5 24.3 %collective-permute-start.2 = (bf16[128,2048]{1,0:T(8,128)(2,1)}, bf16[128,2048]{1,0:T(8,128)(2,1)S(1)}, u32[]{:S(2)}, u32[]{:S(2)}) collective-permute-start(bf16[128,2048]{1,0:T(8,128)(2,1)} %get-tuple-element.1251), channel_id=1, source_target_pairs={{0,32},{32,64},{64,96},{96,128},{128,160},{160,192},{192,224},{1,3... | collective-permute-start | bytes 1572872 | tf_op jit(solution)/shard_map/while/body/eval_jaxpr/ppermute | solution.py:29
  615.3 11.4 collective-permute-start
  617.2 9.5 collective-permute-start.1
  627.7 11.4 collective-permute-start.2
  642.1 9.7 collective-permute-start.3
  644.1 9.3 collective-permute-start.4
  655.5 9.0 collective-permute-start.5
  673.8 17.1 %collective-permute-start.7 = (bf16[128,2048]{1,0:T(8,128)(2,1)S(1)}, bf16[128,2048]{1,0:T(8,128)(2,1)S(1)}, u32[]{:S(2)}, u32[]{:S(2)}) collective-permute-start(bf16[128,2048]{1,0:T(8,128)(2,1)S(1)} %get-tuple-element.1276), channel_id=1, source_target_pairs={{32,0},{64,32},{96,64},{128,96},{160,128},{192,160},{224,192},{33,... | collective-permute-start | bytes 1572872 | tf_op jit(solution)/shard_map/while/body/eval_jaxpr/ppermute | solution.py:29
  694.8 9.6 collective-permute-start.4
  706.5 9.1 collective-permute-start.5
  724.9 11.3 collective-permute-start.7
  769.1 24.6 %collective-permute-start.7 = (bf16[128,2048]{1,0:T(8,128)(2,1)S(1)}, bf16[128,2048]{1,0:T(8,128)(2,1)S(1)}, u32[]{:S(2)}, u32[]{:S(2)}) collective-permute-start(bf16[128,2048]{1,0:T(8,128)(2,1)S(1)} %get-tuple-element.1276), channel_id=1, source_target_pairs={{32,0},{64,32},{96,64},{128,96},{160,128},{192,160},{224,192},{33,... | collective-permute-start | bytes 1572872 | tf_op jit(solution)/shard_map/while/body/eval_jaxpr/ppermute | solution.py:29
  795.6 9.6 collective-permute-start.3
  808.2 9.0 collective-permute-start.5
  826.5 11.2 collective-permute-start.7
  852.2 9.0 collective-permute-start.5
  870.6 16.0 %collective-permute-start.7 = (bf16[128,2048]{1,0:T(8,128)(2,1)S(1)}, bf16[128,2048]{1,0:T(8,128)(2,1)S(1)}, u32[]{:S(2)}, u32[]{:S(2)}) collective-permute-start(bf16[128,2048]{1,0:T(8,128)(2,1)S(1)} %get-tuple-element.1276), channel_id=1, source_target_pairs={{32,0},{64,32},{96,64},{128,96},{160,128},{192,160},{224,192},{33,... | collective-permute-start | bytes 1572872 | tf_op jit(solution)/shard_map/while/body/eval_jaxpr/ppermute | solution.py:29
  890.4 9.2 collective-permute-start.4
  901.7 9.4 collective-permute-start.5
  920.3 178.7 %collective-permute-start.7 = (bf16[128,2048]{1,0:T(8,128)(2,1)S(1)}, bf16[128,2048]{1,0:T(8,128)(2,1)S(1)}, u32[]{:S(2)}, u32[]{:S(2)}) collective-permute-start(bf16[128,2048]{1,0:T(8,128)(2,1)S(1)} %get-tuple-element.1276), channel_id=1, source_target_pairs={{32,0},{64,32},{96,64},{128,96},{160,128},{192,160},{224,192},{33,... | collective-permute-start | bytes 1572872 | tf_op jit(solution)/shard_map/while/body/eval_jaxpr/ppermute | solution.py:29
  1161.5 11.5 collective-permute-start.7
  1235.4 10.5 collective-permute-start.7
  1260.4 9.0 collective-permute-start.5
  1278.8 29.2 %collective-permute-start.7 = (bf16[128,2048]{1,0:T(8,128)(2,1)S(1)}, bf16[128,2048]{1,0:T(8,128)(2,1)S(1)}, u32[]{:S(2)}, u32[]{:S(2)}) collective-permute-start(bf16[128,2048]{1,0:T(8,128)(2,1)S(1)} %get-tuple-element.1276), channel_id=1, source_target_pairs={{32,0},{64,32},{96,64},{128,96},{160,128},{192,160},{224,192},{33,... | collective-permute-start | bytes 1572872 | tf_op jit(solution)/shard_map/while/body/eval_jaxpr/ppermute | solution.py:29
  (78 other events, 334.3 us)
Sparse Core Ops, SparseCore 0:
  10.6 78.3 all-gather.8
  91.5 79.1 all-gather.10
  173.3 79.1 all-gather.12
  254.9 79.1 all-gather.14
where the time goes:
time: 1320 us
  waiting for transfers between devices  710 us (54%)
  starting transfers between devices  363 us (28%)
  other arithmetic  89.5 us (7%)
  local copies, waits for them, and re-layouts  75.9 us (6%)
  matrix products  59.4 us (4%)
  between operations  13.8 us (1%)
    ppermute x18, waiting for transfers between devices, shifted(): return lax.ppermute(block, axis, route)  301 us
    ppermute x27, starting transfers between devices, padded(): lax.ppermute(lax.slice_in_dim(block, block.shape[dim] - width, None, axis...  191 us
    ppermute x18, starting transfers between devices, shifted(): return lax.ppermute(block, axis, route)  120 us
    select_n x45, other arithmetic, put_slot(): jnp.where(active, lax.dynamic_update_index_in_dim(buffer, value, slot, 0)...  83.1 us
    all_gather x1, waiting for transfers between devices, per_device(): lax.all_gather(w_value[0], 'ctx', axis=0, tiled=True)  81.8 us
    all_gather x1, waiting for transfers between devices, per_device(): lax.all_gather(w_key[0], 'ctx', axis=0, tiled=True)  81.8 us
    all_gather x1, waiting for transfers between devices, per_device(): lax.all_gather(w_out[0], 'ctx', axis=0, tiled=True)  81.6 us
    all_gather x1, waiting for transfers between devices, per_device(): lax.all_gather(w_query[0], 'ctx', axis=0, tiled=True)  78 us
  transfers between devices with their start and end apart: 76, of which 49 were waited for; matrix products, arithmetic and copies ran while one was open for 4% of the time, Pallas kernels for 0%

commit v1 on v0

--- a/solution.py
+++ b/solution.py
@@ -99,7 +99,9 @@
     width = HEADS * HDIM
     full_query, full_key, full_value, full_out = (
         lax.all_gather(w_query[0], "ctx", axis=0, tiled=True),
-        lax.all_gather(w_key[0], "ctx", axis=0, tiled=True),
+        jnp.concatenate(
+            lax.all_to_all(jnp.stack([w_key[0]] * lax.axis_size("ctx")), "ctx", 0, 0), axis=0
+        ),
         lax.all_gather(w_value[0], "ctx", axis=0, tiled=True),
         lax.all_gather(w_out[0], "ctx", axis=0, tiled=True),
     )

time: 1320 us -> 1320 us (level)
  starting transfers between devices: 363 us -> 377 us
    all_gather x1 -> x0, waiting for transfers between devices: 81.8 us -> none  [per_device(): lax.all_gather(w_key[0], 'ctx', axis=0, tiled=True)]
    all_gather x1, waiting for transfers between devices: 78 us -> 119 us  [per_device(): lax.all_gather(w_query[0], 'ctx', axis=0, tiled=True)]
    ppermute x18, waiting for transfers between devices: 301 us -> 339 us  [shifted(): return lax.ppermute(block, axis, route)]
    while x54, local copies, waits for them, and re-layouts: 14.1 us -> 0.48 us
  transfers between devices with their start and end apart: 76 -> 76, of which waited for: 49 -> 48; matrix products, arithmetic and copies ran while one was open for 4% -> 3% of each run, Pallas kernels for 0% -> 0%
where the time goes in v1:
time: 1320 us; the launch traced here: 1310 us
  waiting for transfers between devices  702 us (53%)
  starting transfers between devices  377 us (29%)
  other arithmetic  81.4 us (6%)
  local copies, waits for them, and re-layouts  72.3 us (5%)
  matrix products  63.6 us (5%)
  between operations  13.8 us (1%)
    ppermute x18, waiting for transfers between devices, shifted(): return lax.ppermute(block, axis, route)  339 us
    ppermute x27, starting transfers between devices, padded(): lax.ppermute(lax.slice_in_dim(block, block.shape[dim] - width, None, axis...  191 us
    ppermute x18, starting transfers between devices, shifted(): return lax.ppermute(block, axis, route)  125 us
    all_gather x1, waiting for transfers between devices, per_device(): lax.all_gather(w_query[0], 'ctx', axis=0, tiled=True)  119 us
    all_gather x1, waiting for transfers between devices, per_device(): lax.all_gather(w_out[0], 'ctx', axis=0, tiled=True)  81.8 us
    all_gather x1, waiting for transfers between devices, per_device(): lax.all_gather(w_value[0], 'ctx', axis=0, tiled=True)  77.9 us
    select_n x45, other arithmetic, put_slot(): jnp.where(active, lax.dynamic_update_index_in_dim(buffer, value, slot, 0)...  71.4 us
    ppermute x27, waiting for transfers between devices, padded(): lax.ppermute(lax.slice_in_dim(block, 0, width, axis=dim), axis, backward)  68.9 us
  transfers between devices with their start and end apart: 76, of which 48 were waited for; matrix products, arithmetic and copies ran while one was open for 3% of the time, Pallas kernels for 0%

profile of v1, /device:TPU:103, one launch (start us, length us, event | category | flops | bytes accessed | tf_op | source)
XLA Modules:
  0.0 1315.0 jit_solution(4486062442109344808)
XLA Ops:
  12.0 9.8 all-to-all-start
  23.0 118.6 %all-gather.7.cloned.1.call-done = bf16[1,2048,1024]{2,1,0:T(8,128)(2,1)} async-done(((bf16[1,64,1024]{2,1,0:T(8,128)(2,1)}), bf16[1,2048,1024]{2,1,0:T(8,128)(2,1)}) %all-gather.7.cloned.1.call-update) | async-done | bytes 4194320 | tf_op jit(solution)/shard_map/all_gather | solution.py:101
  141.6 77.9 %all-gather.9.cloned.1.call-done = bf16[1,2048,1024]{2,1,0:T(8,128)(2,1)} async-done(((bf16[1,64,1024]{2,1,0:T(8,128)(2,1)}), bf16[1,2048,1024]{2,1,0:T(8,128)(2,1)}) %all-gather.9.cloned.1.call-update) | async-done | bytes 4194320 | tf_op jit(solution)/shard_map/all_gather | solution.py:105
  219.5 81.8 %all-gather.11.cloned.1.call-done = bf16[1,1024,2048]{2,1,0:T(8,128)(2,1)} async-done(((bf16[1,32,2048]{2,1,0:T(8,128)(2,1)}), bf16[1,1024,2048]{2,1,0:T(8,128)(2,1)}) %all-gather.11.cloned.1.call-update) | async-done | bytes 4194320 | tf_op jit(solution)/shard_map/all_gather | solution.py:106
  305.3 306.7 %while.41 = (s32[]{:T(128)}, bf16[128,2048]{1,0:T(8,128)(2,1)}, bf16[2,128,2048]{2,1,0:T(8,128)(2,1)S(1)}, bf16[2,128,2048]{2,1,0:T(8,128)(2,1)}, bf16[2,128,102...) while((s32[]{:T(128)}, bf16[128,2048]{1,0:T(8,128)(2,1)}, ...), condition=%wide.region_9.10_spmd, body=%wide.region_0.9_spmd.sunk | while | flops 2211841024 | bytes 80431864 | solution.py:153
  318.7 7.9 collective-permute-start.2
  328.8 14.7 %collective-permute-done.2 = bf16[128,2048]{1,0:T(8,128)(2,1)} collective-permute-done((bf16[128,2048]{1,0:T(8,128)(2,1)}, bf16[128,2048]{1,0:T(8,128)(2,1)}, u32[]{:S(2)}, u32[]{:S(2)}) %collective-permute-start.2) | collective-permute-done | bytes 524320 | tf_op jit(solution)/shard_map/while/body/eval_jaxpr/ppermute | solution.py:29
  345.0 10.8 conditional.8
  357.9 7.4 collective-permute-start.1
  367.4 7.3 conditional.9
  384.5 10.8 conditional.8
  406.4 7.3 conditional.9
  428.9 7.4 collective-permute-start.1
  439.3 22.2 %collective-permute-start.2 = (bf16[128,2048]{1,0:T(8,128)(2,1)}, bf16[128,2048]{1,0:T(8,128)(2,1)}, u32[]{:S(2)}, u32[]{:S(2)}) collective-permute-start(bf16[128,2048]{1,0:T(8,128)(2,1)} %get-tuple-element.1251), channel_id=1, source_target_pairs={{0,32},{32,64},{64,96},{96,128},{128,160},{160,192},{192,224},{1,3... | collective-permute-start | bytes 1572872 | tf_op jit(solution)/shard_map/while/body/eval_jaxpr/ppermute | solution.py:29
  471.6 7.4 collective-permute-start.1
  497.2 7.4 collective-permute-start.1
  507.6 7.8 collective-permute-start.2
  525.4 7.4 collective-permute-start.1
  551.0 7.4 collective-permute-start.1
  561.5 18.6 %collective-permute-start.2 = (bf16[128,2048]{1,0:T(8,128)(2,1)}, bf16[128,2048]{1,0:T(8,128)(2,1)}, u32[]{:S(2)}, u32[]{:S(2)}) collective-permute-start(bf16[128,2048]{1,0:T(8,128)(2,1)} %get-tuple-element.1251), channel_id=1, source_target_pairs={{0,32},{32,64},{64,96},{96,128},{128,160},{160,192},{192,224},{1,3... | collective-permute-start | bytes 1572872 | tf_op jit(solution)/shard_map/while/body/eval_jaxpr/ppermute | solution.py:29
  590.1 7.4 collective-permute-start.1
  613.2 695.2 %while.42 = (s32[]{:T(128)}, bf16[128,2048]{1,0:T(8,128)(2,1)S(1)}, bf16[2,128,2048]{2,1,0:T(8,128)(2,1)}, s32[]{:T(128)}, bf16[2,2,128,1024]{3,2,1,0:T(8,128)(2...) while((s32[]{:T(128)}, bf16[128,2048]{1,0:T(8,128)(2,1)S(1)}, ...), condition=%wide.region_24.25_spmd, body=%wide.region_10.24_spmd.sunk | while | flops 3389073152 | bytes 146007536 | solution.py:200
  616.3 7.4 collective-permute-start.4
  636.7 7.2 collective-permute-done.6
  648.1 14.5 %collective-permute-done.7 = bf16[128,2048]{1,0:T(8,128)(2,1)S(1)} collective-permute-done((bf16[128,2048]{1,0:T(8,128)(2,1)S(1)}, bf16[128,2048]{1,0:T(8,128)(2,1)S(1)}, u32[]{:S(2)}, u32[]{:S(2)}) %collective-permute-start.7) | collective-permute-done | bytes 524320 | tf_op jit(solution)/shard_map/while/body/eval_jaxpr/ppermute | solution.py:29
  677.4 7.5 collective-permute-start.5
  686.9 7.2 collective-permute-done.6
  698.2 8.6 collective-permute-done.7
  729.6 7.2 collective-permute-done.6
  740.9 24.7 %collective-permute-done.7 = bf16[128,2048]{1,0:T(8,128)(2,1)S(1)} collective-permute-done((bf16[128,2048]{1,0:T(8,128)(2,1)S(1)}, bf16[128,2048]{1,0:T(8,128)(2,1)S(1)}, u32[]{:S(2)}, u32[]{:S(2)}) %collective-permute-start.7) | collective-permute-done | bytes 524320 | tf_op jit(solution)/shard_map/while/body/eval_jaxpr/ppermute | solution.py:29
  788.4 7.2 collective-permute-done.6
  799.7 9.5 collective-permute-done.7
  832.1 7.2 collective-permute-done.6
  843.4 16.5 %collective-permute-done.7 = bf16[128,2048]{1,0:T(8,128)(2,1)S(1)} collective-permute-done((bf16[128,2048]{1,0:T(8,128)(2,1)S(1)}, bf16[128,2048]{1,0:T(8,128)(2,1)S(1)}, u32[]{:S(2)}, u32[]{:S(2)}) %collective-permute-start.7) | collective-permute-done | bytes 524320 | tf_op jit(solution)/shard_map/while/body/eval_jaxpr/ppermute | solution.py:29
  882.7 7.2 collective-permute-done.6
  894.0 197.5 %collective-permute-done.7 = bf16[128,2048]{1,0:T(8,128)(2,1)S(1)} collective-permute-done((bf16[128,2048]{1,0:T(8,128)(2,1)S(1)}, bf16[128,2048]{1,0:T(8,128)(2,1)S(1)}, u32[]{:S(2)}, u32[]{:S(2)}) %collective-permute-start.7) | collective-permute-done | bytes 524320 | tf_op jit(solution)/shard_map/while/body/eval_jaxpr/ppermute | solution.py:29
  1103.2 11.8 conditional.10
  1116.0 7.1 collective-permute-start.5
  1125.1 7.2 collective-permute-done.6
  1132.3 22.2 %conditional.11 = (bf16[128,2048]{1,0:T(8,128)(2,1)S(1)}) conditional(s32[]{:T(128)} %convert_element_type.302, () %tuple.209, (bf16[2,192,1024]{2,1,0:T(8,128)(2,1)S(1)}, bf16[2,32,1024]{2,1,0:T(8,128)(2,1)}, bf16[2,32,1024]{2,1,0:T(8,128)(2,1)}, bf16[2048,1024]{1,0:T(8,128)(2,1)}, bf16[2,128,2048]{2,1,0:T(8,128)(2,1)S(1)}, /*index=5*/s32[]{:T(128)}, ...), branch_computations={%region_15.15_spmd, %region_16.23_spmd} | conditional | flops 2693800704 | bytes 71440024 | solution.py:194
  1158.6 9.5 collective-permute-done.7
  1179.8 11.8 conditional.10
  1192.6 7.1 collective-permute-start.5
  1201.7 7.2 collective-permute-done.6
  1208.9 22.2 %conditional.11 = (bf16[128,2048]{1,0:T(8,128)(2,1)S(1)}) conditional(s32[]{:T(128)} %convert_element_type.302, () %tuple.209, (bf16[2,192,1024]{2,1,0:T(8,128)(2,1)S(1)}, bf16[2,32,1024]{2,1,0:T(8,128)(2,1)}, bf16[2,32,1024]{2,1,0:T(8,128)(2,1)}, bf16[2048,1024]{1,0:T(8,128)(2,1)}, bf16[2,128,2048]{2,1,0:T(8,128)(2,1)S(1)}, /*index=5*/s32[]{:T(128)}, ...), branch_computations={%region_15.15_spmd, %region_16.23_spmd} | conditional | flops 2693800704 | bytes 71440024 | solution.py:194
  1235.1 8.6 collective-permute-done.7
  1266.5 7.2 collective-permute-done.6
  1275.9 31.0 %collective-permute-start.7 = (bf16[128,2048]{1,0:T(8,128)(2,1)S(1)}, bf16[128,2048]{1,0:T(8,128)(2,1)S(1)}, u32[]{:S(2)}, u32[]{:S(2)}) collective-permute-start(bf16[128,2048]{1,0:T(8,128)(2,1)S(1)} %get-tuple-element.1276), channel_id=1, source_target_pairs={{32,0},{64,32},{96,64},{128,96},{160,128},{192,160},{224,192},{33,... | collective-permute-start | bytes 1572872 | tf_op jit(solution)/shard_map/while/body/eval_jaxpr/ppermute | solution.py:29
  (678 shorter events, 485.9 us)
Async XLA Ops:
  7.2 134.4 %all-gather.7.cloned.1.call-start = ((), (), s32[]{:S(2)}) async-start(), calls=%async_computation.1 | async-start | bytes 4325376 | tf_op jit(solution)/shard_map/all_gather | solution.py:101
  7.9 211.6 %all-gather.9.cloned.1.call-start = ((), (), s32[]{:S(2)}) async-start(), calls=%async_computation.2 | async-start | bytes 4325376 | tf_op jit(solution)/shard_map/all_gather | solution.py:105
  12.0 129.6 %all-to-all-start = ((bf16[32,64,1024]{2,1,0:T(8,128)(2,1)}), bf16[32,64,1024]{2,1,0:T(8,128)(2,1)}, u32[]{:S(2)}, u32[]{:S(2)}) async-start(bf16[32,64,1024]{2,1,0:T(8,128)(2,1)} %stack.74), calls=%async_computation | async-start | bytes 8388608 | tf_op jit(solution)/shard_map/all_to_all | solution.py:103
  21.9 279.4 %all-gather.11.cloned.1.call-start = ((), (), s32[]{:S(2)}) async-start(), calls=%async_computation.3 | async-start | bytes 4325376 | tf_op jit(solution)/shard_map/all_gather | solution.py:106
  307.0 10.7 collective-permute-start
  318.7 24.8 %collective-permute-start.2 = (bf16[128,2048]{1,0:T(8,128)(2,1)}, bf16[128,2048]{1,0:T(8,128)(2,1)}, u32[]{:S(2)}, u32[]{:S(2)}) collective-permute-start(bf16[128,2048]{1,0:T(8,128)(2,1)} %get-tuple-element.1251), channel_id=1, source_target_pairs={{0,32},{32,64},{64,96},{96,128},{128,160},{160,192},{192,224},{1,3... | collective-permute-start | bytes 1572872 | tf_op jit(solution)/shard_map/while/body/eval_jaxpr/ppermute | solution.py:29
  355.9 11.4 collective-permute-start
  357.9 9.5 collective-permute-start.1
  395.4 10.9 collective-permute-start
  413.7 11.5 collective-permute-start.2
  426.9 11.4 collective-permute-start
  428.9 9.5 collective-permute-start.1
  439.3 28.6 %collective-permute-start.2 = (bf16[128,2048]{1,0:T(8,128)(2,1)}, bf16[128,2048]{1,0:T(8,128)(2,1)}, u32[]{:S(2)}, u32[]{:S(2)}) collective-permute-start(bf16[128,2048]{1,0:T(8,128)(2,1)} %get-tuple-element.1251), channel_id=1, source_target_pairs={{0,32},{32,64},{64,96},{96,128},{128,160},{160,192},{192,224},{1,3... | collective-permute-start | bytes 1572872 | tf_op jit(solution)/shard_map/while/body/eval_jaxpr/ppermute | solution.py:29
  469.6 11.4 collective-permute-start
  471.6 9.5 collective-permute-start.1
  482.0 11.5 collective-permute-start.2
  495.2 11.4 collective-permute-start
  497.2 9.5 collective-permute-start.1
  507.6 14.2 %collective-permute-start.2 = (bf16[128,2048]{1,0:T(8,128)(2,1)}, bf16[128,2048]{1,0:T(8,128)(2,1)}, u32[]{:S(2)}, u32[]{:S(2)}) collective-permute-start(bf16[128,2048]{1,0:T(8,128)(2,1)} %get-tuple-element.1251), channel_id=1, source_target_pairs={{0,32},{32,64},{64,96},{96,128},{128,160},{160,192},{192,224},{1,3... | collective-permute-start | bytes 1572872 | tf_op jit(solution)/shard_map/while/body/eval_jaxpr/ppermute | solution.py:29
  523.5 11.4 collective-permute-start
  525.4 9.5 collective-permute-start.1
  535.8 11.5 collective-permute-start.2
  549.1 11.4 collective-permute-start
  551.0 9.5 collective-permute-start.1
  561.5 25.0 %collective-permute-start.2 = (bf16[128,2048]{1,0:T(8,128)(2,1)}, bf16[128,2048]{1,0:T(8,128)(2,1)}, u32[]{:S(2)}, u32[]{:S(2)}) collective-permute-start(bf16[128,2048]{1,0:T(8,128)(2,1)} %get-tuple-element.1251), channel_id=1, source_target_pairs={{0,32},{32,64},{64,96},{96,128},{128,160},{160,192},{192,224},{1,3... | collective-permute-start | bytes 1572872 | tf_op jit(solution)/shard_map/while/body/eval_jaxpr/ppermute | solution.py:29
  588.2 11.4 collective-permute-start
  590.1 9.5 collective-permute-start.1
  600.5 11.5 collective-permute-start.2
  614.3 9.7 collective-permute-start.3
  616.3 9.3 collective-permute-start.4
  634.8 9.1 collective-permute-start.6
  646.1 16.4 %collective-permute-start.7 = (bf16[128,2048]{1,0:T(8,128)(2,1)S(1)}, bf16[128,2048]{1,0:T(8,128)(2,1)S(1)}, u32[]{:S(2)}, u32[]{:S(2)}) collective-permute-start(bf16[128,2048]{1,0:T(8,128)(2,1)S(1)} %get-tuple-element.1276), channel_id=1, source_target_pairs={{32,0},{64,32},{96,64},{128,96},{160,128},{192,160},{224,192},{33,... | collective-permute-start | bytes 1572872 | tf_op jit(solution)/shard_map/while/body/eval_jaxpr/ppermute | solution.py:29
  665.6 9.7 collective-permute-start.4
  677.4 9.5 collective-permute-start.5
  684.9 9.1 collective-permute-start.6
  696.3 10.5 collective-permute-start.7
  727.6 9.1 collective-permute-start.6
  739.0 26.6 %collective-permute-start.7 = (bf16[128,2048]{1,0:T(8,128)(2,1)S(1)}, bf16[128,2048]{1,0:T(8,128)(2,1)S(1)}, u32[]{:S(2)}, u32[]{:S(2)}) collective-permute-start(bf16[128,2048]{1,0:T(8,128)(2,1)S(1)} %get-tuple-element.1276), channel_id=1, source_target_pairs={{32,0},{64,32},{96,64},{128,96},{160,128},{192,160},{224,192},{33,... | collective-permute-start | bytes 1572872 | tf_op jit(solution)/shard_map/while/body/eval_jaxpr/ppermute | solution.py:29
  766.7 9.5 collective-permute-start.3
  786.5 9.1 collective-permute-start.6
  797.8 11.5 collective-permute-start.7
  830.1 9.1 collective-permute-start.6
  841.5 18.5 %collective-permute-start.7 = (bf16[128,2048]{1,0:T(8,128)(2,1)S(1)}, bf16[128,2048]{1,0:T(8,128)(2,1)S(1)}, u32[]{:S(2)}, u32[]{:S(2)}) collective-permute-start(bf16[128,2048]{1,0:T(8,128)(2,1)S(1)} %get-tuple-element.1276), channel_id=1, source_target_pairs={{32,0},{64,32},{96,64},{128,96},{160,128},{192,160},{224,192},{33,... | collective-permute-start | bytes 1572872 | tf_op jit(solution)/shard_map/while/body/eval_jaxpr/ppermute | solution.py:29
  880.8 9.1 collective-permute-start.6
  892.1 199.4 %collective-permute-start.7 = (bf16[128,2048]{1,0:T(8,128)(2,1)S(1)}, bf16[128,2048]{1,0:T(8,128)(2,1)S(1)}, u32[]{:S(2)}, u32[]{:S(2)}) collective-permute-start(bf16[128,2048]{1,0:T(8,128)(2,1)S(1)} %get-tuple-element.1276), channel_id=1, source_target_pairs={{32,0},{64,32},{96,64},{128,96},{160,128},{192,160},{224,192},{33,... | collective-permute-start | bytes 1572872 | tf_op jit(solution)/shard_map/while/body/eval_jaxpr/ppermute | solution.py:29
  1156.6 11.5 collective-permute-start.7
  1233.2 10.5 collective-permute-start.7
  1275.9 32.5 %collective-permute-start.7 = (bf16[128,2048]{1,0:T(8,128)(2,1)S(1)}, bf16[128,2048]{1,0:T(8,128)(2,1)S(1)}, u32[]{:S(2)}, u32[]{:S(2)}) collective-permute-start(bf16[128,2048]{1,0:T(8,128)(2,1)S(1)} %get-tuple-element.1276), channel_id=1, source_target_pairs={{32,0},{64,32},{96,64},{128,96},{160,128},{192,160},{224,192},{33,... | collective-permute-start | bytes 1572872 | tf_op jit(solution)/shard_map/while/body/eval_jaxpr/ppermute | solution.py:29
  (69 other events, 483.6 us)
Sparse Core Ops, SparseCore 0:
  10.6 130.9 all-gather.6
  144.2 75.2 all-gather.8
  222.1 79.1 all-gather.10
